TPU v7x, 512 devices: a whole 4x4x16 slice. The times are simulated.
512 devices in a mesh: chain: 128 (over z, y, core), seg: 4 (over x).
Axes of the slice: x: 4, y: 4, z: 16, core: 2. Of those that a mesh axis runs over, the one named last changes fastest.
Arguments:
- band_tiles: bfloat16 [128, 1024, 7, 1024], P('chain', None, None, 'seg'), may hold values from -0.009765625 to 0.009765625
- widths: int32 [128], P('chain'), may hold values from 2 to 6, as said below
- warm_start: float32 [131072, 256], P(('chain', 'seg')), may hold values from -4 to 4
- scores: float32 [131072, 64], P(('chain', 'seg')), may hold values from -6 to 6
- penalty: float32 [256], replicated, may hold values from 0.05 to 0.5
Outputs:
- fitted_effects: float32 [131072, 256], P(('chain', 'seg'))
Inputs may be any that keep to these rules, and one draw needn't show every extreme that they name: `widths`: each block uses between 2 and 6 forward tiles; both 2 and 6 occur in every draw.
All inputs are finite; a program needn't handle non-finite values.
Results may differ from a plain program's by a relative error of at most 0.00085.
Values may be sent and summed in bfloat16 or wider, within the bound.
No kernel may reach another device: no remote copies, remote signals or barrier semaphores. Data moves between devices by JAX's collectives and lax.ppermute only.
A program may use at most 64 MiB of HBM per device.

v0:
```python
import jax
import jax.numpy as jnp
from jax import lax
from jax.sharding import PartitionSpec as P

ITERS = 2
step_size = 0.8


def shifted(value, axis, by):
    length = lax.axis_size(axis)
    pairs = [(i, i + by) for i in range(length) if 0 <= i + by < length]
    return lax.ppermute(value, axis, pairs)


def soft_limit(values, limit):
    return jnp.sign(values) * jnp.maximum(jnp.abs(values) - limit, 0.0)


def per_device(band_tiles, widths, warm_start, scores, penalty):
    local_tiles = band_tiles[0]
    block_len = local_tiles.shape[0]
    depth = local_tiles.shape[1]
    strip_len = local_tiles.shape[2]
    flat_tiles = local_tiles.reshape(block_len, depth * strip_len)
    columns = warm_start.shape[1]
    path_len = columns // scores.shape[1]
    target = jnp.tile(scores, (1, path_len))
    offsets = jnp.arange(depth, dtype=jnp.int32)
    live_flags = offsets <= widths[0]
    live_half = live_flags.astype(jnp.bfloat16)
    live_full = live_flags.astype(jnp.float32)
    estimate = warm_start
    for iteration in range(ITERS):
        current = estimate.astype(jnp.bfloat16)
        whole_block = lax.all_gather(current, "seg", axis=0, tiled=True)
        ahead_list = [current] + [
            shifted(current, "chain", -shift_by) for shift_by in range(1, depth)
        ]
        stacked = (jnp.stack(ahead_list) * live_half[:, None, None]).reshape(
            depth * strip_len, columns
        )

        def forward_term(start_row, count, stacked=stacked):
            return jnp.dot(flat_tiles, stacked, preferred_element_type=jnp.float32)

        forward = lax.psum_scatter(
            forward_term(jnp.int32(0), strip_len * lax.axis_size("seg")).astype(jnp.bfloat16),
            "seg",
            scatter_dimension=0,
            tiled=True,
        ).astype(jnp.float32)
        outgoing = lax.dot_general(
            flat_tiles, whole_block, (((0,), (0,)), ((), ())), preferred_element_type=jnp.float32
        )
        outgoing = outgoing.reshape(depth, strip_len, columns) * live_full[:, None, None]
        backward = outgoing[0]
        for shift_by in range(1, depth):
            backward = backward + shifted(
                outgoing[shift_by].astype(jnp.bfloat16), "chain", shift_by
            ).astype(jnp.float32)
        stepped = estimate - step_size * (estimate + (forward + backward) - target)
        estimate = soft_limit(stepped, step_size * penalty)
    return estimate


def solution(mesh):
    in_specs = (
        P("chain", None, None, "seg"),
        P("chain"),
        P(("chain", "seg"), None),
        P(("chain", "seg"), None),
        P(),
    )
    out_specs = P(("chain", "seg"), None)
    return jax.shard_map(
        per_device, mesh=mesh, in_specs=in_specs, out_specs=out_specs, check_vma=False
    )
```

profile of v0, /device:TPU:65, one launch (start us, length us, event | category | flops | bytes accessed | tf_op | source)
XLA Modules:
  0.0 180.1 jit_solution(8785533673903158669)
XLA Ops:
  7.7 2.7 %collective-permute-start.5 = (bf16[256,256]{0,1:T(8,128)(2,1)S(1)}, bf16[256,256]{0,1:T(8,128)(2,1)S(1)}, u32[]{:S(2)}, u32[]{:S(2)}) collective-permute-start(bf16[256,256]{0,1:T(8,128)(2,1)S(1)} %get-tuple-element.10), channel_id=1, source_target_pairs={{24,0},{28,4},{32,8},{36,12},{40,16},{44,20},{48,24},{52,28},{56,3... | collective-permute-start | bytes 393224 | tf_op jit(solution)/shard_map/ppermute | solution.py:13
  10.4 4.9 %collective-permute-start.4 = (bf16[256,256]{0,1:T(8,128)(2,1)S(1)}, bf16[256,256]{0,1:T(8,128)(2,1)S(1)}, u32[]{:S(2)}, u32[]{:S(2)}) collective-permute-start(bf16[256,256]{0,1:T(8,128)(2,1)S(1)} %get-tuple-element.10), channel_id=1, source_target_pairs={{20,0},{24,4},{28,8},{32,12},{36,16},{40,20},{44,24},{48,28},{52,3... | collective-permute-start | bytes 393224 | tf_op jit(solution)/shard_map/ppermute | solution.py:13
  15.3 2.3 %collective-permute-start.3 = (bf16[256,256]{0,1:T(8,128)(2,1)S(1)}, bf16[256,256]{0,1:T(8,128)(2,1)S(1)}, u32[]{:S(2)}, u32[]{:S(2)}) collective-permute-start(bf16[256,256]{0,1:T(8,128)(2,1)S(1)} %get-tuple-element.10), channel_id=1, source_target_pairs={{16,0},{20,4},{24,8},{28,12},{32,16},{36,20},{40,24},{44,28},{48,3... | collective-permute-start | bytes 393224 | tf_op jit(solution)/shard_map/ppermute | solution.py:13
  17.6 2.9 %collective-permute-start.2 = (bf16[256,256]{0,1:T(8,128)(2,1)S(1)}, bf16[256,256]{0,1:T(8,128)(2,1)S(1)}, u32[]{:S(2)}, u32[]{:S(2)}) collective-permute-start(bf16[256,256]{0,1:T(8,128)(2,1)S(1)} %get-tuple-element.10), channel_id=1, source_target_pairs={{12,0},{16,4},{20,8},{24,12},{28,16},{32,20},{36,24},{40,28},{44,3... | collective-permute-start | bytes 393224 | tf_op jit(solution)/shard_map/ppermute | solution.py:13
  20.5 2.0 %collective-permute-start = (bf16[256,256]{0,1:T(8,128)(2,1)S(1)}, bf16[256,256]{0,1:T(8,128)(2,1)S(1)}, u32[]{:S(2)}, u32[]{:S(2)}) collective-permute-start(bf16[256,256]{0,1:T(8,128)(2,1)S(1)} %get-tuple-element.10), channel_id=1, source_target_pairs={{4,0},{8,4},{12,8},{16,12},{20,16},{24,20},{28,24},{32,28},{36,32}... | collective-permute-start | bytes 393224 | tf_op jit(solution)/shard_map/ppermute | solution.py:13
  22.5 10.2 %all_gather.6 = bf16[1024,256]{0,1:T(8,128)(2,1)S(1)} all-gather(bf16[256,256]{0,1:T(8,128)(2,1)S(1)} %get-tuple-element.10), channel_id=1, replica_groups=mesh['chain'=128,'seg'=4] {'seg'}, dimensions={0}, use_global_device_ids=true | all-gather | bytes 655360 | tf_op jit(solution)/shard_map/all_gather | solution.py:36
  33.4 6.1 %copy.14 = bf16[1,1024,7,256]{1,3,2,0:T(8,128)(2,1)} copy(bf16[1,1024,7,256]{3,1,2,0:T(8,128)(2,1)} %param.5) | data formatting | bytes 7340032 | tf_op args[0]
  39.5 8.1 %collective-permute-start.1 = (bf16[256,256]{0,1:T(8,128)(2,1)S(1)}, bf16[256,256]{0,1:T(8,128)(2,1)S(1)}, u32[]{:S(2)}, u32[]{:S(2)}) collective-permute-start(bf16[256,256]{0,1:T(8,128)(2,1)S(1)} %get-tuple-element.10), channel_id=1, source_target_pairs={{8,0},{12,4},{16,8},{20,12},{24,16},{28,20},{32,24},{36,28},{40,32... | collective-permute-start | bytes 393224 | tf_op jit(solution)/shard_map/ppermute | solution.py:13
  47.7 2.9 %collective-permute-done.1 = bf16[256,256]{0,1:T(8,128)(2,1)S(1)} collective-permute-done((bf16[256,256]{0,1:T(8,128)(2,1)S(1)}, bf16[256,256]{0,1:T(8,128)(2,1)S(1)}, u32[]{:S(2)}, u32[]{:S(2)}) %collective-permute-start.1) | collective-permute-done | bytes 131104 | tf_op jit(solution)/shard_map/ppermute | solution.py:13
  51.4 4.0 %fusion.5 = bf16[1024,256]{0,1:T(8,128)(2,1)} fusion(bf16[1792,256]{1,0:T(8,128)(2,1)S(1)} %bitcast.149, bf16[1024,1792]{0,1:T(8,128)(2,1)} %bitcast.145), kind=kOutput, calls=%fused_computation.6 | convolution fusion | flops 939786240 | bytes 5111808 | tf_op jit(solution)/shard_map/dot_general | solution.py:45
  55.5 3.2 %fusion.29 = (bf16[7,256,256]{1,2,0:T(8,128)(2,1)S(1)}, f32[7,256,256]{1,2,0:T(8,128)S(1)}) fusion(f32[7]{0:T(128)S(1)} %compare_convert_fusion, bf16[1024,256]{0,1:T(8,128)(2,1)S(1)} %all_gather.6, bf16[1,1024,7,256]{1,3,2,0:T(8,128)(2,1)} %copy.14), kind=kOutput, calls=%fused_computation.68 | convolution fusion | flops 940441600 | bytes 6946844 | tf_op jit(solution)/shard_map/dot_general | solution.py:53
  58.8 7.5 %collective-permute-start.6 = (bf16[256,256]{0,1:T(8,128)(2,1)S(1)}, bf16[256,256]{0,1:T(8,128)(2,1)S(1)}, u32[]{:S(2)}, u32[]{:S(2)}) collective-permute-start(bf16[256,256]{0,1:T(8,128)(2,1)S(1)} %get-tuple-element.17), channel_id=1, source_target_pairs={{0,4},{4,8},{8,12},{12,16},{16,20},{20,24},{24,28},{28,32},{32,36}... | collective-permute-start | bytes 393224 | tf_op jit(solution)/shard_map/ppermute | solution.py:13
  70.2 4.1 %collective-permute-start.9 = (bf16[256,256]{0,1:T(8,128)(2,1)S(1)}, bf16[256,256]{0,1:T(8,128)(2,1)S(1)}, u32[]{:S(2)}, u32[]{:S(2)}) collective-permute-start(bf16[256,256]{0,1:T(8,128)(2,1)S(1)} %get-tuple-element.20), channel_id=1, source_target_pairs={{0,16},{4,20},{8,24},{12,28},{16,32},{20,36},{24,40},{28,44},{32,4... | collective-permute-start | bytes 393224 | tf_op jit(solution)/shard_map/ppermute | solution.py:13
  74.3 5.4 %collective-permute-start.8 = (bf16[256,256]{0,1:T(8,128)(2,1)S(1)}, bf16[256,256]{0,1:T(8,128)(2,1)S(1)}, u32[]{:S(2)}, u32[]{:S(2)}) collective-permute-start(bf16[256,256]{0,1:T(8,128)(2,1)S(1)} %get-tuple-element.21), channel_id=1, source_target_pairs={{0,12},{4,16},{8,20},{12,24},{16,28},{20,32},{24,36},{28,40},{32,4... | collective-permute-start | bytes 393224 | tf_op jit(solution)/shard_map/ppermute | solution.py:13
  79.6 4.1 %collective-permute-start.7 = (bf16[256,256]{0,1:T(8,128)(2,1)S(1)}, bf16[256,256]{0,1:T(8,128)(2,1)S(1)}, u32[]{:S(2)}, u32[]{:S(2)}) collective-permute-start(bf16[256,256]{0,1:T(8,128)(2,1)S(1)} %get-tuple-element.22), channel_id=1, source_target_pairs={{0,8},{4,12},{8,16},{12,20},{16,24},{20,28},{24,32},{28,36},{32,40... | collective-permute-start | bytes 393224 | tf_op jit(solution)/shard_map/ppermute | solution.py:13
  85.3 3.4 %collective-permute-done.7 = bf16[256,256]{0,1:T(8,128)(2,1)S(1)} collective-permute-done((bf16[256,256]{0,1:T(8,128)(2,1)S(1)}, bf16[256,256]{0,1:T(8,128)(2,1)S(1)}, u32[]{:S(2)}, u32[]{:S(2)}) %collective-permute-start.7) | collective-permute-done | bytes 131104 | tf_op jit(solution)/shard_map/ppermute | solution.py:13
  89.9 2.6 %collective-permute-start.17 = (bf16[256,256]{0,1:T(8,128)(2,1)S(1)}, bf16[256,256]{0,1:T(8,128)(2,1)S(1)}, u32[]{:S(2)}, u32[]{:S(2)}) collective-permute-start(bf16[256,256]{0,1:T(8,128)(2,1)S(1)} %get-tuple-element.6), channel_id=1, source_target_pairs={{24,0},{28,4},{32,8},{36,12},{40,16},{44,20},{48,24},{52,28},{56,3... | collective-permute-start | bytes 393224 | tf_op jit(solution)/shard_map/ppermute | solution.py:13
  92.6 7.3 %collective-permute-start.16 = (bf16[256,256]{0,1:T(8,128)(2,1)S(1)}, bf16[256,256]{0,1:T(8,128)(2,1)S(1)}, u32[]{:S(2)}, u32[]{:S(2)}) collective-permute-start(bf16[256,256]{0,1:T(8,128)(2,1)S(1)} %get-tuple-element.6), channel_id=1, source_target_pairs={{20,0},{24,4},{28,8},{32,12},{36,16},{40,20},{44,24},{48,28},{52,3... | collective-permute-start | bytes 393224 | tf_op jit(solution)/shard_map/ppermute | solution.py:13
  99.9 2.5 %collective-permute-start.15 = (bf16[256,256]{0,1:T(8,128)(2,1)S(1)}, bf16[256,256]{0,1:T(8,128)(2,1)S(1)}, u32[]{:S(2)}, u32[]{:S(2)}) collective-permute-start(bf16[256,256]{0,1:T(8,128)(2,1)S(1)} %get-tuple-element.6), channel_id=1, source_target_pairs={{16,0},{20,4},{24,8},{28,12},{32,16},{36,20},{40,24},{44,28},{48,3... | collective-permute-start | bytes 393224 | tf_op jit(solution)/shard_map/ppermute | solution.py:13
  102.4 2.9 %collective-permute-start.14 = (bf16[256,256]{0,1:T(8,128)(2,1)S(1)}, bf16[256,256]{0,1:T(8,128)(2,1)S(1)}, u32[]{:S(2)}, u32[]{:S(2)}) collective-permute-start(bf16[256,256]{0,1:T(8,128)(2,1)S(1)} %get-tuple-element.6), channel_id=1, source_target_pairs={{12,0},{16,4},{20,8},{24,12},{28,16},{32,20},{36,24},{40,28},{44,3... | collective-permute-start | bytes 393224 | tf_op jit(solution)/shard_map/ppermute | solution.py:13
  105.3 2.0 %collective-permute-start.12 = (bf16[256,256]{0,1:T(8,128)(2,1)S(1)}, bf16[256,256]{0,1:T(8,128)(2,1)S(1)}, u32[]{:S(2)}, u32[]{:S(2)}) collective-permute-start(bf16[256,256]{0,1:T(8,128)(2,1)S(1)} %get-tuple-element.6), channel_id=1, source_target_pairs={{4,0},{8,4},{12,8},{16,12},{20,16},{24,20},{28,24},{32,28},{36,32}... | collective-permute-start | bytes 393224 | tf_op jit(solution)/shard_map/ppermute | solution.py:13
  107.3 9.9 %all_gather.7 = bf16[1024,256]{0,1:T(8,128)(2,1)S(1)} all-gather(bf16[256,256]{0,1:T(8,128)(2,1)S(1)} %get-tuple-element.6), channel_id=1, replica_groups=mesh['chain'=128,'seg'=4] {'seg'}, dimensions={0}, use_global_device_ids=true | all-gather | bytes 655360 | tf_op jit(solution)/shard_map/all_gather | solution.py:36
  117.2 3.2 %collective-permute-start.13 = (bf16[256,256]{0,1:T(8,128)(2,1)S(1)}, bf16[256,256]{0,1:T(8,128)(2,1)S(1)}, u32[]{:S(2)}, u32[]{:S(2)}) collective-permute-start(bf16[256,256]{0,1:T(8,128)(2,1)S(1)} %get-tuple-element.6), channel_id=1, source_target_pairs={{8,0},{12,4},{16,8},{20,12},{24,16},{28,20},{32,24},{36,28},{40,32... | collective-permute-start | bytes 393224 | tf_op jit(solution)/shard_map/ppermute | solution.py:13
  120.5 2.5 %collective-permute-done.13 = bf16[256,256]{0,1:T(8,128)(2,1)S(1)} collective-permute-done((bf16[256,256]{0,1:T(8,128)(2,1)S(1)}, bf16[256,256]{0,1:T(8,128)(2,1)S(1)}, u32[]{:S(2)}, u32[]{:S(2)}) %collective-permute-start.13) | collective-permute-done | bytes 131104 | tf_op jit(solution)/shard_map/ppermute | solution.py:13
  123.8 4.0 %fusion.6 = bf16[1024,256]{0,1:T(8,128)(2,1)} fusion(bf16[1792,256]{1,0:T(8,128)(2,1)S(1)} %bitcast.150, bf16[1024,1792]{0,1:T(8,128)(2,1)} %bitcast.146), kind=kOutput, calls=%fused_computation.7 | convolution fusion | flops 939786240 | bytes 5111808 | tf_op jit(solution)/shard_map/dot_general | solution.py:45
  127.8 3.2 %convolution_bitcast_fusion = f32[1792,256]{0,1:T(8,128)S(1)} fusion(bf16[1024,256]{0,1:T(8,128)(2,1)S(1)} %all_gather.7, bf16[1024,1792]{0,1:T(8,128)(2,1)} %bitcast.147), kind=kOutput, calls=%fused_computation.2 | convolution fusion | flops 939524096 | bytes 6029312 | tf_op jit(solution)/shard_map/dot_general | solution.py:53
  136.2 8.0 %collective-permute-start.18 = (bf16[256,256]{0,1:T(8,128)(2,1)S(1)}, bf16[256,256]{0,1:T(8,128)(2,1)S(1)}, u32[]{:S(2)}, u32[]{:S(2)}) collective-permute-start(bf16[256,256]{0,1:T(8,128)(2,1)S(1)} %get-tuple-element.11), channel_id=1, source_target_pairs={{0,4},{4,8},{8,12},{12,16},{16,20},{20,24},{24,28},{28,32},{32,36}... | collective-permute-start | bytes 393224 | tf_op jit(solution)/shard_map/ppermute | solution.py:13
  144.2 5.8 %collective-permute-start.23 = (bf16[256,256]{0,1:T(8,128)(2,1)S(1)}, bf16[256,256]{0,1:T(8,128)(2,1)S(1)}, u32[]{:S(2)}, u32[]{:S(2)}) collective-permute-start(bf16[256,256]{0,1:T(8,128)(2,1)S(1)} %get-tuple-element.12), channel_id=1, source_target_pairs={{0,24},{4,28},{8,32},{12,36},{16,40},{20,44},{24,48},{28,52},{32,5... | collective-permute-start | bytes 393224 | tf_op jit(solution)/shard_map/ppermute | solution.py:13
  151.9 4.9 %collective-permute-start.21 = (bf16[256,256]{0,1:T(8,128)(2,1)S(1)}, bf16[256,256]{0,1:T(8,128)(2,1)S(1)}, u32[]{:S(2)}, u32[]{:S(2)}) collective-permute-start(bf16[256,256]{0,1:T(8,128)(2,1)S(1)} %get-tuple-element.14), channel_id=1, source_target_pairs={{0,16},{4,20},{8,24},{12,28},{16,32},{20,36},{24,40},{28,44},{32,4... | collective-permute-start | bytes 393224 | tf_op jit(solution)/shard_map/ppermute | solution.py:13
  156.8 5.6 %collective-permute-start.20 = (bf16[256,256]{0,1:T(8,128)(2,1)S(1)}, bf16[256,256]{0,1:T(8,128)(2,1)S(1)}, u32[]{:S(2)}, u32[]{:S(2)}) collective-permute-start(bf16[256,256]{0,1:T(8,128)(2,1)S(1)} %get-tuple-element.15), channel_id=1, source_target_pairs={{0,12},{4,16},{8,20},{12,24},{16,28},{20,32},{24,36},{28,40},{32,4... | collective-permute-start | bytes 393224 | tf_op jit(solution)/shard_map/ppermute | solution.py:13
  162.5 3.8 %collective-permute-start.19 = (bf16[256,256]{0,1:T(8,128)(2,1)S(1)}, bf16[256,256]{0,1:T(8,128)(2,1)S(1)}, u32[]{:S(2)}, u32[]{:S(2)}) collective-permute-start(bf16[256,256]{0,1:T(8,128)(2,1)S(1)} %get-tuple-element.16), channel_id=1, source_target_pairs={{0,8},{4,12},{8,16},{12,20},{16,24},{20,28},{24,32},{28,36},{32,40... | collective-permute-start | bytes 393224 | tf_op jit(solution)/shard_map/ppermute | solution.py:13
  168.1 3.1 %collective-permute-done.19 = bf16[256,256]{0,1:T(8,128)(2,1)S(1)} collective-permute-done((bf16[256,256]{0,1:T(8,128)(2,1)S(1)}, bf16[256,256]{0,1:T(8,128)(2,1)S(1)}, u32[]{:S(2)}, u32[]{:S(2)}) %collective-permute-start.19) | collective-permute-done | bytes 131104 | tf_op jit(solution)/shard_map/ppermute | solution.py:13
  (62 shorter events, 20.4 us)
Async XLA Ops:
  6.5 82.2 %reduce-scatter.3.cloned.1.call-start = ((), (), s32[]{:S(2)}) async-start(), calls=%async_computation.2 | async-start | bytes 655360 | tf_op jit(solution)/shard_map/reduce_scatter | solution.py:47
  7.7 43.0 %collective-permute-start.5 = (bf16[256,256]{0,1:T(8,128)(2,1)S(1)}, bf16[256,256]{0,1:T(8,128)(2,1)S(1)}, u32[]{:S(2)}, u32[]{:S(2)}) collective-permute-start(bf16[256,256]{0,1:T(8,128)(2,1)S(1)} %get-tuple-element.10), channel_id=1, source_target_pairs={{24,0},{28,4},{32,8},{36,12},{40,16},{44,20},{48,24},{52,28},{56,3... | collective-permute-start | bytes 393224 | tf_op jit(solution)/shard_map/ppermute | solution.py:13
  10.4 40.2 %collective-permute-start.4 = (bf16[256,256]{0,1:T(8,128)(2,1)S(1)}, bf16[256,256]{0,1:T(8,128)(2,1)S(1)}, u32[]{:S(2)}, u32[]{:S(2)}) collective-permute-start(bf16[256,256]{0,1:T(8,128)(2,1)S(1)} %get-tuple-element.10), channel_id=1, source_target_pairs={{20,0},{24,4},{28,8},{32,12},{36,16},{40,20},{44,24},{48,28},{52,3... | collective-permute-start | bytes 393224 | tf_op jit(solution)/shard_map/ppermute | solution.py:13
  15.3 35.3 %collective-permute-start.3 = (bf16[256,256]{0,1:T(8,128)(2,1)S(1)}, bf16[256,256]{0,1:T(8,128)(2,1)S(1)}, u32[]{:S(2)}, u32[]{:S(2)}) collective-permute-start(bf16[256,256]{0,1:T(8,128)(2,1)S(1)} %get-tuple-element.10), channel_id=1, source_target_pairs={{16,0},{20,4},{24,8},{28,12},{32,16},{36,20},{40,24},{44,28},{48,3... | collective-permute-start | bytes 393224 | tf_op jit(solution)/shard_map/ppermute | solution.py:13
  17.6 33.0 %collective-permute-start.2 = (bf16[256,256]{0,1:T(8,128)(2,1)S(1)}, bf16[256,256]{0,1:T(8,128)(2,1)S(1)}, u32[]{:S(2)}, u32[]{:S(2)}) collective-permute-start(bf16[256,256]{0,1:T(8,128)(2,1)S(1)} %get-tuple-element.10), channel_id=1, source_target_pairs={{12,0},{16,4},{20,8},{24,12},{28,16},{32,20},{36,24},{40,28},{44,3... | collective-permute-start | bytes 393224 | tf_op jit(solution)/shard_map/ppermute | solution.py:13
  20.5 19.0 %collective-permute-start = (bf16[256,256]{0,1:T(8,128)(2,1)S(1)}, bf16[256,256]{0,1:T(8,128)(2,1)S(1)}, u32[]{:S(2)}, u32[]{:S(2)}) collective-permute-start(bf16[256,256]{0,1:T(8,128)(2,1)S(1)} %get-tuple-element.10), channel_id=1, source_target_pairs={{4,0},{8,4},{12,8},{16,12},{20,16},{24,20},{28,24},{32,28},{36,32}... | collective-permute-start | bytes 393224 | tf_op jit(solution)/shard_map/ppermute | solution.py:13
  39.5 11.0 %collective-permute-start.1 = (bf16[256,256]{0,1:T(8,128)(2,1)S(1)}, bf16[256,256]{0,1:T(8,128)(2,1)S(1)}, u32[]{:S(2)}, u32[]{:S(2)}) collective-permute-start(bf16[256,256]{0,1:T(8,128)(2,1)S(1)} %get-tuple-element.10), channel_id=1, source_target_pairs={{8,0},{12,4},{16,8},{20,12},{24,16},{28,20},{32,24},{36,28},{40,32... | collective-permute-start | bytes 393224 | tf_op jit(solution)/shard_map/ppermute | solution.py:13
  55.4 115.8 %reduce-scatter.5.cloned.1.call-start = ((), (), s32[]{:S(2)}) async-start(), calls=%async_computation.3 | async-start | bytes 655360 | tf_op jit(solution)/shard_map/reduce_scatter | solution.py:47
  55.5 28.3 %copy-start.1 = (f32[256]{0:T(256)S(1)}, f32[256]{0:T(256)}, u32[]{:S(2)}) copy-start(f32[256]{0:T(256)} %param.9) | copy-start | bytes 3076
  55.5 33.2 %copy-start = (f32[256,64]{0,1:T(8,128)S(1)}, f32[256,64]{0,1:T(8,128)}, u32[]{:S(2)}) copy-start(f32[256,64]{0,1:T(8,128)} %param.8) | copy-start | bytes 196612
  58.8 20.8 %collective-permute-start.6 = (bf16[256,256]{0,1:T(8,128)(2,1)S(1)}, bf16[256,256]{0,1:T(8,128)(2,1)S(1)}, u32[]{:S(2)}, u32[]{:S(2)}) collective-permute-start(bf16[256,256]{0,1:T(8,128)(2,1)S(1)} %get-tuple-element.17), channel_id=1, source_target_pairs={{0,4},{4,8},{8,12},{12,16},{16,20},{20,24},{24,28},{28,32},{32,36}... | collective-permute-start | bytes 393224 | tf_op jit(solution)/shard_map/ppermute | solution.py:13
  66.3 17.5 %collective-permute-start.11 = (bf16[256,256]{0,1:T(8,128)(2,1)S(1)}, bf16[256,256]{0,1:T(8,128)(2,1)S(1)}, u32[]{:S(2)}, u32[]{:S(2)}) collective-permute-start(bf16[256,256]{0,1:T(8,128)(2,1)S(1)} %get-tuple-element.18), channel_id=1, source_target_pairs={{0,24},{4,28},{8,32},{12,36},{16,40},{20,44},{24,48},{28,52},{32,5... | collective-permute-start | bytes 393224 | tf_op jit(solution)/shard_map/ppermute | solution.py:13
  68.2 15.6 %collective-permute-start.10 = (bf16[256,256]{0,1:T(8,128)(2,1)S(1)}, bf16[256,256]{0,1:T(8,128)(2,1)S(1)}, u32[]{:S(2)}, u32[]{:S(2)}) collective-permute-start(bf16[256,256]{0,1:T(8,128)(2,1)S(1)} %get-tuple-element.19), channel_id=1, source_target_pairs={{0,20},{4,24},{8,28},{12,32},{16,36},{20,40},{24,44},{28,48},{32,5... | collective-permute-start | bytes 393224 | tf_op jit(solution)/shard_map/ppermute | solution.py:13
  70.2 13.6 %collective-permute-start.9 = (bf16[256,256]{0,1:T(8,128)(2,1)S(1)}, bf16[256,256]{0,1:T(8,128)(2,1)S(1)}, u32[]{:S(2)}, u32[]{:S(2)}) collective-permute-start(bf16[256,256]{0,1:T(8,128)(2,1)S(1)} %get-tuple-element.20), channel_id=1, source_target_pairs={{0,16},{4,20},{8,24},{12,28},{16,32},{20,36},{24,40},{28,44},{32,4... | collective-permute-start | bytes 393224 | tf_op jit(solution)/shard_map/ppermute | solution.py:13
  74.3 11.0 %collective-permute-start.8 = (bf16[256,256]{0,1:T(8,128)(2,1)S(1)}, bf16[256,256]{0,1:T(8,128)(2,1)S(1)}, u32[]{:S(2)}, u32[]{:S(2)}) collective-permute-start(bf16[256,256]{0,1:T(8,128)(2,1)S(1)} %get-tuple-element.21), channel_id=1, source_target_pairs={{0,12},{4,16},{8,20},{12,24},{16,28},{20,32},{24,36},{28,40},{32,4... | collective-permute-start | bytes 393224 | tf_op jit(solution)/shard_map/ppermute | solution.py:13
  79.6 9.1 %collective-permute-start.7 = (bf16[256,256]{0,1:T(8,128)(2,1)S(1)}, bf16[256,256]{0,1:T(8,128)(2,1)S(1)}, u32[]{:S(2)}, u32[]{:S(2)}) collective-permute-start(bf16[256,256]{0,1:T(8,128)(2,1)S(1)} %get-tuple-element.22), channel_id=1, source_target_pairs={{0,8},{4,12},{8,16},{12,20},{16,24},{20,28},{24,32},{28,36},{32,40... | collective-permute-start | bytes 393224 | tf_op jit(solution)/shard_map/ppermute | solution.py:13
  89.9 33.1 %collective-permute-start.17 = (bf16[256,256]{0,1:T(8,128)(2,1)S(1)}, bf16[256,256]{0,1:T(8,128)(2,1)S(1)}, u32[]{:S(2)}, u32[]{:S(2)}) collective-permute-start(bf16[256,256]{0,1:T(8,128)(2,1)S(1)} %get-tuple-element.6), channel_id=1, source_target_pairs={{24,0},{28,4},{32,8},{36,12},{40,16},{44,20},{48,24},{52,28},{56,3... | collective-permute-start | bytes 393224 | tf_op jit(solution)/shard_map/ppermute | solution.py:13
  92.6 30.5 %collective-permute-start.16 = (bf16[256,256]{0,1:T(8,128)(2,1)S(1)}, bf16[256,256]{0,1:T(8,128)(2,1)S(1)}, u32[]{:S(2)}, u32[]{:S(2)}) collective-permute-start(bf16[256,256]{0,1:T(8,128)(2,1)S(1)} %get-tuple-element.6), channel_id=1, source_target_pairs={{20,0},{24,4},{28,8},{32,12},{36,16},{40,20},{44,24},{48,28},{52,3... | collective-permute-start | bytes 393224 | tf_op jit(solution)/shard_map/ppermute | solution.py:13
  99.9 23.1 %collective-permute-start.15 = (bf16[256,256]{0,1:T(8,128)(2,1)S(1)}, bf16[256,256]{0,1:T(8,128)(2,1)S(1)}, u32[]{:S(2)}, u32[]{:S(2)}) collective-permute-start(bf16[256,256]{0,1:T(8,128)(2,1)S(1)} %get-tuple-element.6), channel_id=1, source_target_pairs={{16,0},{20,4},{24,8},{28,12},{32,16},{36,20},{40,24},{44,28},{48,3... | collective-permute-start | bytes 393224 | tf_op jit(solution)/shard_map/ppermute | solution.py:13
  102.4 20.6 %collective-permute-start.14 = (bf16[256,256]{0,1:T(8,128)(2,1)S(1)}, bf16[256,256]{0,1:T(8,128)(2,1)S(1)}, u32[]{:S(2)}, u32[]{:S(2)}) collective-permute-start(bf16[256,256]{0,1:T(8,128)(2,1)S(1)} %get-tuple-element.6), channel_id=1, source_target_pairs={{12,0},{16,4},{20,8},{24,12},{28,16},{32,20},{36,24},{40,28},{44,3... | collective-permute-start | bytes 393224 | tf_op jit(solution)/shard_map/ppermute | solution.py:13
  105.3 11.9 %collective-permute-start.12 = (bf16[256,256]{0,1:T(8,128)(2,1)S(1)}, bf16[256,256]{0,1:T(8,128)(2,1)S(1)}, u32[]{:S(2)}, u32[]{:S(2)}) collective-permute-start(bf16[256,256]{0,1:T(8,128)(2,1)S(1)} %get-tuple-element.6), channel_id=1, source_target_pairs={{4,0},{8,4},{12,8},{16,12},{20,16},{24,20},{28,24},{32,28},{36,32}... | collective-permute-start | bytes 393224 | tf_op jit(solution)/shard_map/ppermute | solution.py:13
  117.2 5.7 %collective-permute-start.13 = (bf16[256,256]{0,1:T(8,128)(2,1)S(1)}, bf16[256,256]{0,1:T(8,128)(2,1)S(1)}, u32[]{:S(2)}, u32[]{:S(2)}) collective-permute-start(bf16[256,256]{0,1:T(8,128)(2,1)S(1)} %get-tuple-element.6), channel_id=1, source_target_pairs={{8,0},{12,4},{16,8},{20,12},{24,16},{28,20},{32,24},{36,28},{40,32... | collective-permute-start | bytes 393224 | tf_op jit(solution)/shard_map/ppermute | solution.py:13
  136.2 26.3 %collective-permute-start.18 = (bf16[256,256]{0,1:T(8,128)(2,1)S(1)}, bf16[256,256]{0,1:T(8,128)(2,1)S(1)}, u32[]{:S(2)}, u32[]{:S(2)}) collective-permute-start(bf16[256,256]{0,1:T(8,128)(2,1)S(1)} %get-tuple-element.11), channel_id=1, source_target_pairs={{0,4},{4,8},{8,12},{12,16},{16,20},{20,24},{24,28},{28,32},{32,36}... | collective-permute-start | bytes 393224 | tf_op jit(solution)/shard_map/ppermute | solution.py:13
  144.2 22.0 %collective-permute-start.23 = (bf16[256,256]{0,1:T(8,128)(2,1)S(1)}, bf16[256,256]{0,1:T(8,128)(2,1)S(1)}, u32[]{:S(2)}, u32[]{:S(2)}) collective-permute-start(bf16[256,256]{0,1:T(8,128)(2,1)S(1)} %get-tuple-element.12), channel_id=1, source_target_pairs={{0,24},{4,28},{8,32},{12,36},{16,40},{20,44},{24,48},{28,52},{32,5... | collective-permute-start | bytes 393224 | tf_op jit(solution)/shard_map/ppermute | solution.py:13
  150.0 16.3 %collective-permute-start.22 = (bf16[256,256]{0,1:T(8,128)(2,1)S(1)}, bf16[256,256]{0,1:T(8,128)(2,1)S(1)}, u32[]{:S(2)}, u32[]{:S(2)}) collective-permute-start(bf16[256,256]{0,1:T(8,128)(2,1)S(1)} %get-tuple-element.13), channel_id=1, source_target_pairs={{0,20},{4,24},{8,28},{12,32},{16,36},{20,40},{24,44},{28,48},{32,5... | collective-permute-start | bytes 393224 | tf_op jit(solution)/shard_map/ppermute | solution.py:13
  151.9 14.3 %collective-permute-start.21 = (bf16[256,256]{0,1:T(8,128)(2,1)S(1)}, bf16[256,256]{0,1:T(8,128)(2,1)S(1)}, u32[]{:S(2)}, u32[]{:S(2)}) collective-permute-start(bf16[256,256]{0,1:T(8,128)(2,1)S(1)} %get-tuple-element.14), channel_id=1, source_target_pairs={{0,16},{4,20},{8,24},{12,28},{16,32},{20,36},{24,40},{28,44},{32,4... | collective-permute-start | bytes 393224 | tf_op jit(solution)/shard_map/ppermute | solution.py:13
  156.8 11.3 %collective-permute-start.20 = (bf16[256,256]{0,1:T(8,128)(2,1)S(1)}, bf16[256,256]{0,1:T(8,128)(2,1)S(1)}, u32[]{:S(2)}, u32[]{:S(2)}) collective-permute-start(bf16[256,256]{0,1:T(8,128)(2,1)S(1)} %get-tuple-element.15), channel_id=1, source_target_pairs={{0,12},{4,16},{8,20},{12,24},{16,28},{20,32},{24,36},{28,40},{32,4... | collective-permute-start | bytes 393224 | tf_op jit(solution)/shard_map/ppermute | solution.py:13
  162.5 8.7 %collective-permute-start.19 = (bf16[256,256]{0,1:T(8,128)(2,1)S(1)}, bf16[256,256]{0,1:T(8,128)(2,1)S(1)}, u32[]{:S(2)}, u32[]{:S(2)}) collective-permute-start(bf16[256,256]{0,1:T(8,128)(2,1)S(1)} %get-tuple-element.16), channel_id=1, source_target_pairs={{0,8},{4,12},{8,16},{12,20},{16,24},{20,28},{24,32},{28,36},{32,40... | collective-permute-start | bytes 393224 | tf_op jit(solution)/shard_map/ppermute | solution.py:13
Sparse Core Ops, SparseCore 0:
  55.6 32.8 reduce-scatter.2
  128.0 33.7 reduce-scatter.4
where the time goes:
time: 181 us; the launch traced here: 180 us
  starting transfers between devices  98.5 us (54%)
  blocking collectives  20.1 us (11%)
  waiting for transfers between devices  15.3 us (8%)
  between operations  14.6 us (8%)
  matrix products  14.4 us (8%)
  local copies, waits for them, and re-layouts  13 us (7%)
  other arithmetic  4.26 us (2%)
    ppermute x24, starting transfers between devices, shifted(): return lax.ppermute(value, axis, pairs)  98.4 us
    all_gather x2, blocking collectives, per_device(): whole_block = lax.all_gather(current, 'seg', axis=0, tiled=True)  20.1 us
    ppermute x24, waiting for transfers between devices, shifted(): return lax.ppermute(value, axis, pairs)  15.3 us
    dot_general x2, matrix products, forward_term(): return jnp.dot(flat_tiles, stacked, preferred_element_type=jnp.float32)  7.95 us
    unnamed x16, local copies, waits for them, and re-layouts  7.27 us
    dot_general x2, matrix products, per_device(): lax.dot_general(flat_tiles, whole_block, (((0,), (0,)), ((), ())), prefer...  6.41 us
  transfers between devices with their start and end apart: 26, of which 6 were waited for; matrix products, arithmetic and copies ran while one was open for 10% of the time, Pallas kernels for 0%

commit v1 on v0

--- a/solution.py
+++ b/solution.py
@@ -5,6 +5,14 @@
 
 ITERS = 2
 step_size = 0.8
+
+
+def gather_from_all(value, axis, dim):
+    size = lax.axis_size(axis)
+    repeats = [size if d == dim else 1 for d in range(value.ndim)]
+    return lax.all_to_all(
+        jnp.tile(value, repeats), axis, split_axis=dim, concat_axis=dim, tiled=True
+    )
 
 
 def shifted(value, axis, by):
@@ -33,7 +41,7 @@
     estimate = warm_start
     for iteration in range(ITERS):
         current = estimate.astype(jnp.bfloat16)
-        whole_block = lax.all_gather(current, "seg", axis=0, tiled=True)
+        whole_block = gather_from_all(current, "seg", 0)
         ahead_list = [current] + [
             shifted(current, "chain", -shift_by) for shift_by in range(1, depth)
         ]

time: 181 us -> 167 us (0.923)
  the two profiles are of different devices: /device:TPU:65 before, /device:TPU:67 now
where the time goes in v1:
time: 167 us; the launch traced here: 165 us
  starting transfers between devices  97.5 us (58%)
  waiting for transfers between devices  18.5 us (11%)
  local copies, waits for them, and re-layouts  15.6 us (9%)
  between operations  14.7 us (9%)
  matrix products  14.6 us (9%)
  other arithmetic  4.59 us (3%)
    ppermute x24, starting transfers between devices, shifted(): return lax.ppermute(value, axis, pairs)  86.7 us
    ppermute x24, waiting for transfers between devices, shifted(): return lax.ppermute(value, axis, pairs)  18.5 us
    all_to_all x2, starting transfers between devices, gather_from_all(): lax.all_to_all(jnp.tile(value, repeats), axis, split_axis=dim, concat_axi...  10.8 us
    dot_general x2, matrix products, forward_term(): return jnp.dot(flat_tiles, stacked, preferred_element_type=jnp.float32)  7.98 us
    unnamed x28, local copies, waits for them, and re-layouts  7.98 us
    dot_general x2, matrix products, per_device(): lax.dot_general(flat_tiles, whole_block, (((0,), (0,)), ((), ())), prefer...  6.6 us
  transfers between devices with their start and end apart: 28, of which 5 were waited for; matrix products, arithmetic and copies ran while one was open for 18% of the time, Pallas kernels for 0%

profile of v1, /device:TPU:67, one launch (start us, length us, event | category | flops | bytes accessed | tf_op | source)
XLA Modules:
  0.0 165.5 jit_solution(18043006639418743032)
XLA Ops:
  7.7 2.6 %collective-permute-start = (bf16[256,256]{0,1:T(8,128)(2,1)S(1)}, bf16[256,256]{0,1:T(8,128)(2,1)S(1)}, u32[]{:S(2)}, u32[]{:S(2)}) collective-permute-start(bf16[256,256]{0,1:T(8,128)(2,1)S(1)} %get-tuple-element.10), channel_id=1, source_target_pairs={{4,0},{8,4},{12,8},{16,12},{20,16},{24,20},{28,24},{32,28},{36,32}... | collective-permute-start | bytes 393224 | tf_op jit(solution)/shard_map/ppermute | solution.py:21
  10.2 2.7 %collective-permute-start.5 = (bf16[256,256]{0,1:T(8,128)(2,1)S(1)}, bf16[256,256]{0,1:T(8,128)(2,1)S(1)}, u32[]{:S(2)}, u32[]{:S(2)}) collective-permute-start(bf16[256,256]{0,1:T(8,128)(2,1)S(1)} %get-tuple-element.10), channel_id=1, source_target_pairs={{24,0},{28,4},{32,8},{36,12},{40,16},{44,20},{48,24},{52,28},{56,3... | collective-permute-start | bytes 393224 | tf_op jit(solution)/shard_map/ppermute | solution.py:21
  13.0 4.4 %collective-permute-start.4 = (bf16[256,256]{0,1:T(8,128)(2,1)S(1)}, bf16[256,256]{0,1:T(8,128)(2,1)S(1)}, u32[]{:S(2)}, u32[]{:S(2)}) collective-permute-start(bf16[256,256]{0,1:T(8,128)(2,1)S(1)} %get-tuple-element.10), channel_id=1, source_target_pairs={{20,0},{24,4},{28,8},{32,12},{36,16},{40,20},{44,24},{48,28},{52,3... | collective-permute-start | bytes 393224 | tf_op jit(solution)/shard_map/ppermute | solution.py:21
  17.4 3.0 %collective-permute-start.3 = (bf16[256,256]{0,1:T(8,128)(2,1)S(1)}, bf16[256,256]{0,1:T(8,128)(2,1)S(1)}, u32[]{:S(2)}, u32[]{:S(2)}) collective-permute-start(bf16[256,256]{0,1:T(8,128)(2,1)S(1)} %get-tuple-element.10), channel_id=1, source_target_pairs={{16,0},{20,4},{24,8},{28,12},{32,16},{36,20},{40,24},{44,28},{48,3... | collective-permute-start | bytes 393224 | tf_op jit(solution)/shard_map/ppermute | solution.py:21
  20.4 2.0 %collective-permute-start.2 = (bf16[256,256]{0,1:T(8,128)(2,1)S(1)}, bf16[256,256]{0,1:T(8,128)(2,1)S(1)}, u32[]{:S(2)}, u32[]{:S(2)}) collective-permute-start(bf16[256,256]{0,1:T(8,128)(2,1)S(1)} %get-tuple-element.10), channel_id=1, source_target_pairs={{12,0},{16,4},{20,8},{24,12},{28,16},{32,20},{36,24},{40,28},{44,3... | collective-permute-start | bytes 393224 | tf_op jit(solution)/shard_map/ppermute | solution.py:21
  23.4 4.3 %all-to-all-start = ((bf16[4,256,256]{2,1,0:T(8,128)(2,1)}), bf16[4,256,256]{2,1,0:T(8,128)(2,1)S(1)}, u32[]{:S(2)}, u32[]{:S(2)}) async-start(bf16[4,256,256]{2,1,0:T(8,128)(2,1)} %tile.8), calls=%async_computation.1 | async-start | bytes 1048576 | tf_op jit(solution)/shard_map/all_to_all | solution.py:13
  28.3 6.1 %copy.15 = bf16[1,1024,7,256]{1,3,2,0:T(8,128)(2,1)} copy(bf16[1,1024,7,256]{3,1,2,0:T(8,128)(2,1)} %param.5) | data formatting | bytes 7340032 | tf_op args[0]
  34.5 6.4 %collective-permute-start.1 = (bf16[256,256]{0,1:T(8,128)(2,1)S(1)}, bf16[256,256]{0,1:T(8,128)(2,1)S(1)}, u32[]{:S(2)}, u32[]{:S(2)}) collective-permute-start(bf16[256,256]{0,1:T(8,128)(2,1)S(1)} %get-tuple-element.10), channel_id=1, source_target_pairs={{8,0},{12,4},{16,8},{20,12},{24,16},{28,20},{32,24},{36,28},{40,32... | collective-permute-start | bytes 393224 | tf_op jit(solution)/shard_map/ppermute | solution.py:21
  40.9 3.8 %collective-permute-done.1 = bf16[256,256]{0,1:T(8,128)(2,1)S(1)} collective-permute-done((bf16[256,256]{0,1:T(8,128)(2,1)S(1)}, bf16[256,256]{0,1:T(8,128)(2,1)S(1)}, u32[]{:S(2)}, u32[]{:S(2)}) %collective-permute-start.1) | collective-permute-done | bytes 131104 | tf_op jit(solution)/shard_map/ppermute | solution.py:21
  45.7 4.0 %fusion.5 = bf16[1024,256]{0,1:T(8,128)(2,1)} fusion(bf16[1792,256]{1,0:T(8,128)(2,1)S(1)} %bitcast.150, bf16[1024,1792]{0,1:T(8,128)(2,1)} %bitcast.145), kind=kOutput, calls=%fused_computation.6 | convolution fusion | flops 939786240 | bytes 5111808 | tf_op jit(solution)/shard_map/dot_general | solution.py:53
  49.7 3.2 %fusion.28 = (bf16[7,256,256]{1,2,0:T(8,128)(2,1)S(1)}, f32[7,256,256]{1,2,0:T(8,128)S(1)}) fusion(f32[7]{0:T(128)S(1)} %compare_convert_fusion, bf16[1024,256,1]{1,0,2:T(8,128)(2,1)S(1)} %bitcast.149, bf16[1,1024,7,256]{1,3,2,0:T(8,128)(2,1)} %copy.15), kind=kOutput, calls=%fused_computation.67 | convolution fusion | flops 940441600 | bytes 6946844 | tf_op jit(solution)/shard_map/dot_general | solution.py:61
  53.0 4.5 %collective-permute-start.6 = (bf16[256,256]{0,1:T(8,128)(2,1)S(1)}, bf16[256,256]{0,1:T(8,128)(2,1)S(1)}, u32[]{:S(2)}, u32[]{:S(2)}) collective-permute-start(bf16[256,256]{0,1:T(8,128)(2,1)S(1)} %get-tuple-element.17), channel_id=1, source_target_pairs={{0,4},{4,8},{8,12},{12,16},{16,20},{20,24},{24,28},{28,32},{32,36}... | collective-permute-start | bytes 393224 | tf_op jit(solution)/shard_map/ppermute | solution.py:21
  57.5 2.1 %collective-permute-start.11 = (bf16[256,256]{0,1:T(8,128)(2,1)S(1)}, bf16[256,256]{0,1:T(8,128)(2,1)S(1)}, u32[]{:S(2)}, u32[]{:S(2)}) collective-permute-start(bf16[256,256]{0,1:T(8,128)(2,1)S(1)} %get-tuple-element.18), channel_id=1, source_target_pairs={{0,24},{4,28},{8,32},{12,36},{16,40},{20,44},{24,48},{28,52},{32,5... | collective-permute-start | bytes 393224 | tf_op jit(solution)/shard_map/ppermute | solution.py:21
  61.5 5.3 %collective-permute-start.9 = (bf16[256,256]{0,1:T(8,128)(2,1)S(1)}, bf16[256,256]{0,1:T(8,128)(2,1)S(1)}, u32[]{:S(2)}, u32[]{:S(2)}) collective-permute-start(bf16[256,256]{0,1:T(8,128)(2,1)S(1)} %get-tuple-element.20), channel_id=1, source_target_pairs={{0,16},{4,20},{8,24},{12,28},{16,32},{20,36},{24,40},{28,44},{32,4... | collective-permute-start | bytes 393224 | tf_op jit(solution)/shard_map/ppermute | solution.py:21
  66.9 5.3 %collective-permute-start.8 = (bf16[256,256]{0,1:T(8,128)(2,1)S(1)}, bf16[256,256]{0,1:T(8,128)(2,1)S(1)}, u32[]{:S(2)}, u32[]{:S(2)}) collective-permute-start(bf16[256,256]{0,1:T(8,128)(2,1)S(1)} %get-tuple-element.21), channel_id=1, source_target_pairs={{0,12},{4,16},{8,20},{12,24},{16,28},{20,32},{24,36},{28,40},{32,4... | collective-permute-start | bytes 393224 | tf_op jit(solution)/shard_map/ppermute | solution.py:21
  72.2 4.1 %collective-permute-start.7 = (bf16[256,256]{0,1:T(8,128)(2,1)S(1)}, bf16[256,256]{0,1:T(8,128)(2,1)S(1)}, u32[]{:S(2)}, u32[]{:S(2)}) collective-permute-start(bf16[256,256]{0,1:T(8,128)(2,1)S(1)} %get-tuple-element.22), channel_id=1, source_target_pairs={{0,8},{4,12},{8,16},{12,20},{16,24},{20,28},{24,32},{28,36},{32,40... | collective-permute-start | bytes 393224 | tf_op jit(solution)/shard_map/ppermute | solution.py:21
  76.5 4.9 %collective-permute-done.7 = bf16[256,256]{0,1:T(8,128)(2,1)S(1)} collective-permute-done((bf16[256,256]{0,1:T(8,128)(2,1)S(1)}, bf16[256,256]{0,1:T(8,128)(2,1)S(1)}, u32[]{:S(2)}, u32[]{:S(2)}) %collective-permute-start.7) | collective-permute-done | bytes 131104 | tf_op jit(solution)/shard_map/ppermute | solution.py:21
  83.6 2.3 %collective-permute-start.12 = (bf16[256,256]{0,1:T(8,128)(2,1)S(1)}, bf16[256,256]{0,1:T(8,128)(2,1)S(1)}, u32[]{:S(2)}, u32[]{:S(2)}) collective-permute-start(bf16[256,256]{0,1:T(8,128)(2,1)S(1)} %get-tuple-element.6), channel_id=1, source_target_pairs={{4,0},{8,4},{12,8},{16,12},{20,16},{24,20},{28,24},{32,28},{36,32}... | collective-permute-start | bytes 393224 | tf_op jit(solution)/shard_map/ppermute | solution.py:21
  86.0 2.6 %collective-permute-start.17 = (bf16[256,256]{0,1:T(8,128)(2,1)S(1)}, bf16[256,256]{0,1:T(8,128)(2,1)S(1)}, u32[]{:S(2)}, u32[]{:S(2)}) collective-permute-start(bf16[256,256]{0,1:T(8,128)(2,1)S(1)} %get-tuple-element.6), channel_id=1, source_target_pairs={{24,0},{28,4},{32,8},{36,12},{40,16},{44,20},{48,24},{52,28},{56,3... | collective-permute-start | bytes 393224 | tf_op jit(solution)/shard_map/ppermute | solution.py:21
  88.5 4.5 %collective-permute-start.16 = (bf16[256,256]{0,1:T(8,128)(2,1)S(1)}, bf16[256,256]{0,1:T(8,128)(2,1)S(1)}, u32[]{:S(2)}, u32[]{:S(2)}) collective-permute-start(bf16[256,256]{0,1:T(8,128)(2,1)S(1)} %get-tuple-element.6), channel_id=1, source_target_pairs={{20,0},{24,4},{28,8},{32,12},{36,16},{40,20},{44,24},{48,28},{52,3... | collective-permute-start | bytes 393224 | tf_op jit(solution)/shard_map/ppermute | solution.py:21
  93.0 2.4 %collective-permute-start.15 = (bf16[256,256]{0,1:T(8,128)(2,1)S(1)}, bf16[256,256]{0,1:T(8,128)(2,1)S(1)}, u32[]{:S(2)}, u32[]{:S(2)}) collective-permute-start(bf16[256,256]{0,1:T(8,128)(2,1)S(1)} %get-tuple-element.6), channel_id=1, source_target_pairs={{16,0},{20,4},{24,8},{28,12},{32,16},{36,20},{40,24},{44,28},{48,3... | collective-permute-start | bytes 393224 | tf_op jit(solution)/shard_map/ppermute | solution.py:21
  95.4 2.8 %collective-permute-start.14 = (bf16[256,256]{0,1:T(8,128)(2,1)S(1)}, bf16[256,256]{0,1:T(8,128)(2,1)S(1)}, u32[]{:S(2)}, u32[]{:S(2)}) collective-permute-start(bf16[256,256]{0,1:T(8,128)(2,1)S(1)} %get-tuple-element.6), channel_id=1, source_target_pairs={{12,0},{16,4},{20,8},{24,12},{28,16},{32,20},{36,24},{40,28},{44,3... | collective-permute-start | bytes 393224 | tf_op jit(solution)/shard_map/ppermute | solution.py:21
  99.2 6.5 %all-to-all-start.1 = ((bf16[4,256,256]{2,1,0:T(8,128)(2,1)}), bf16[4,256,256]{2,1,0:T(8,128)(2,1)}, u32[]{:S(2)}, u32[]{:S(2)}) async-start(bf16[4,256,256]{2,1,0:T(8,128)(2,1)} %tile.11), calls=%async_computation.3 | async-start | bytes 1048576 | tf_op jit(solution)/shard_map/all_to_all | solution.py:13
  107.6 4.6 %collective-permute-done.13 = bf16[256,256]{0,1:T(8,128)(2,1)S(1)} collective-permute-done((bf16[256,256]{0,1:T(8,128)(2,1)S(1)}, bf16[256,256]{0,1:T(8,128)(2,1)S(1)}, u32[]{:S(2)}, u32[]{:S(2)}) %collective-permute-start.13) | collective-permute-done | bytes 131104 | tf_op jit(solution)/shard_map/ppermute | solution.py:21
  113.1 4.0 %fusion.6 = bf16[1024,256]{0,1:T(8,128)(2,1)} fusion(bf16[1792,256]{1,0:T(8,128)(2,1)S(1)} %bitcast.151, bf16[1024,1792]{0,1:T(8,128)(2,1)} %bitcast.146), kind=kOutput, calls=%fused_computation.7 | convolution fusion | flops 939786240 | bytes 5111808 | tf_op jit(solution)/shard_map/dot_general | solution.py:53
  117.2 3.4 %convolution_bitcast_fusion = f32[1792,256]{0,1:T(8,128)S(1)} fusion(bf16[1024,256]{1,0:T(8,128)(2,1)} %bitcast.32, bf16[1024,1792]{0,1:T(8,128)(2,1)} %bitcast.147), kind=kOutput, calls=%fused_computation.2 | convolution fusion | flops 939524096 | bytes 6029312 | tf_op jit(solution)/shard_map/dot_general | solution.py:61
  125.7 3.6 %collective-permute-start.18 = (bf16[256,256]{0,1:T(8,128)(2,1)S(1)}, bf16[256,256]{0,1:T(8,128)(2,1)S(1)}, u32[]{:S(2)}, u32[]{:S(2)}) collective-permute-start(bf16[256,256]{0,1:T(8,128)(2,1)S(1)} %get-tuple-element.11), channel_id=1, source_target_pairs={{0,4},{4,8},{8,12},{12,16},{16,20},{20,24},{24,28},{28,32},{32,36}... | collective-permute-start | bytes 393224 | tf_op jit(solution)/shard_map/ppermute | solution.py:21
  129.2 6.1 %collective-permute-start.23 = (bf16[256,256]{0,1:T(8,128)(2,1)S(1)}, bf16[256,256]{0,1:T(8,128)(2,1)S(1)}, u32[]{:S(2)}, u32[]{:S(2)}) collective-permute-start(bf16[256,256]{0,1:T(8,128)(2,1)S(1)} %get-tuple-element.12), channel_id=1, source_target_pairs={{0,24},{4,28},{8,32},{12,36},{16,40},{20,44},{24,48},{28,52},{32,5... | collective-permute-start | bytes 393224 | tf_op jit(solution)/shard_map/ppermute | solution.py:21
  137.3 4.9 %collective-permute-start.21 = (bf16[256,256]{0,1:T(8,128)(2,1)S(1)}, bf16[256,256]{0,1:T(8,128)(2,1)S(1)}, u32[]{:S(2)}, u32[]{:S(2)}) collective-permute-start(bf16[256,256]{0,1:T(8,128)(2,1)S(1)} %get-tuple-element.14), channel_id=1, source_target_pairs={{0,16},{4,20},{8,24},{12,28},{16,32},{20,36},{24,40},{28,44},{32,4... | collective-permute-start | bytes 393224 | tf_op jit(solution)/shard_map/ppermute | solution.py:21
  142.1 5.7 %collective-permute-start.20 = (bf16[256,256]{0,1:T(8,128)(2,1)S(1)}, bf16[256,256]{0,1:T(8,128)(2,1)S(1)}, u32[]{:S(2)}, u32[]{:S(2)}) collective-permute-start(bf16[256,256]{0,1:T(8,128)(2,1)S(1)} %get-tuple-element.15), channel_id=1, source_target_pairs={{0,12},{4,16},{8,20},{12,24},{16,28},{20,32},{24,36},{28,40},{32,4... | collective-permute-start | bytes 393224 | tf_op jit(solution)/shard_map/ppermute | solution.py:21
  147.8 3.6 %collective-permute-start.19 = (bf16[256,256]{0,1:T(8,128)(2,1)S(1)}, bf16[256,256]{0,1:T(8,128)(2,1)S(1)}, u32[]{:S(2)}, u32[]{:S(2)}) collective-permute-start(bf16[256,256]{0,1:T(8,128)(2,1)S(1)} %get-tuple-element.16), channel_id=1, source_target_pairs={{0,8},{4,12},{8,16},{12,20},{16,24},{20,28},{24,32},{28,36},{32,40... | collective-permute-start | bytes 393224 | tf_op jit(solution)/shard_map/ppermute | solution.py:21
  153.5 3.0 %collective-permute-done.19 = bf16[256,256]{0,1:T(8,128)(2,1)S(1)} collective-permute-done((bf16[256,256]{0,1:T(8,128)(2,1)S(1)}, bf16[256,256]{0,1:T(8,128)(2,1)S(1)}, u32[]{:S(2)}, u32[]{:S(2)}) %collective-permute-start.19) | collective-permute-done | bytes 131104 | tf_op jit(solution)/shard_map/ppermute | solution.py:21
  (80 shorter events, 21.9 us)
Async XLA Ops:
  7.7 26.8 %collective-permute-start = (bf16[256,256]{0,1:T(8,128)(2,1)S(1)}, bf16[256,256]{0,1:T(8,128)(2,1)S(1)}, u32[]{:S(2)}, u32[]{:S(2)}) collective-permute-start(bf16[256,256]{0,1:T(8,128)(2,1)S(1)} %get-tuple-element.10), channel_id=1, source_target_pairs={{4,0},{8,4},{12,8},{16,12},{20,16},{24,20},{28,24},{32,28},{36,32}... | collective-permute-start | bytes 393224 | tf_op jit(solution)/shard_map/ppermute | solution.py:21
  10.2 34.6 %collective-permute-start.5 = (bf16[256,256]{0,1:T(8,128)(2,1)S(1)}, bf16[256,256]{0,1:T(8,128)(2,1)S(1)}, u32[]{:S(2)}, u32[]{:S(2)}) collective-permute-start(bf16[256,256]{0,1:T(8,128)(2,1)S(1)} %get-tuple-element.10), channel_id=1, source_target_pairs={{24,0},{28,4},{32,8},{36,12},{40,16},{44,20},{48,24},{52,28},{56,3... | collective-permute-start | bytes 393224 | tf_op jit(solution)/shard_map/ppermute | solution.py:21
  13.0 31.8 %collective-permute-start.4 = (bf16[256,256]{0,1:T(8,128)(2,1)S(1)}, bf16[256,256]{0,1:T(8,128)(2,1)S(1)}, u32[]{:S(2)}, u32[]{:S(2)}) collective-permute-start(bf16[256,256]{0,1:T(8,128)(2,1)S(1)} %get-tuple-element.10), channel_id=1, source_target_pairs={{20,0},{24,4},{28,8},{32,12},{36,16},{40,20},{44,24},{48,28},{52,3... | collective-permute-start | bytes 393224 | tf_op jit(solution)/shard_map/ppermute | solution.py:21
  17.4 27.4 %collective-permute-start.3 = (bf16[256,256]{0,1:T(8,128)(2,1)S(1)}, bf16[256,256]{0,1:T(8,128)(2,1)S(1)}, u32[]{:S(2)}, u32[]{:S(2)}) collective-permute-start(bf16[256,256]{0,1:T(8,128)(2,1)S(1)} %get-tuple-element.10), channel_id=1, source_target_pairs={{16,0},{20,4},{24,8},{28,12},{32,16},{36,20},{40,24},{44,28},{48,3... | collective-permute-start | bytes 393224 | tf_op jit(solution)/shard_map/ppermute | solution.py:21
  20.4 24.4 %collective-permute-start.2 = (bf16[256,256]{0,1:T(8,128)(2,1)S(1)}, bf16[256,256]{0,1:T(8,128)(2,1)S(1)}, u32[]{:S(2)}, u32[]{:S(2)}) collective-permute-start(bf16[256,256]{0,1:T(8,128)(2,1)S(1)} %get-tuple-element.10), channel_id=1, source_target_pairs={{12,0},{16,4},{20,8},{24,12},{28,16},{32,20},{36,24},{40,28},{44,3... | collective-permute-start | bytes 393224 | tf_op jit(solution)/shard_map/ppermute | solution.py:21
  23.4 26.3 %all-to-all-start = ((bf16[4,256,256]{2,1,0:T(8,128)(2,1)}), bf16[4,256,256]{2,1,0:T(8,128)(2,1)S(1)}, u32[]{:S(2)}, u32[]{:S(2)}) async-start(bf16[4,256,256]{2,1,0:T(8,128)(2,1)} %tile.8), calls=%async_computation.1 | async-start | bytes 1048576 | tf_op jit(solution)/shard_map/all_to_all | solution.py:13
  27.7 53.7 %reduce-scatter.3.cloned.1.call-start = ((), (), s32[]{:S(2)}) async-start(), calls=%async_computation.4 | async-start | bytes 655360 | tf_op jit(solution)/shard_map/reduce_scatter | solution.py:55
  34.5 10.3 %collective-permute-start.1 = (bf16[256,256]{0,1:T(8,128)(2,1)S(1)}, bf16[256,256]{0,1:T(8,128)(2,1)S(1)}, u32[]{:S(2)}, u32[]{:S(2)}) collective-permute-start(bf16[256,256]{0,1:T(8,128)(2,1)S(1)} %get-tuple-element.10), channel_id=1, source_target_pairs={{8,0},{12,4},{16,8},{20,12},{24,16},{28,20},{32,24},{36,28},{40,32... | collective-permute-start | bytes 393224 | tf_op jit(solution)/shard_map/ppermute | solution.py:21
  49.7 26.7 %copy-start.7 = (f32[256]{0:T(256)S(1)}, f32[256]{0:T(256)}, u32[]{:S(2)}) copy-start(f32[256]{0:T(256)} %param.9) | copy-start | bytes 3076
  49.7 32.3 %copy-start = (f32[256,64]{0,1:T(8,128)S(1)}, f32[256,64]{0,1:T(8,128)}, u32[]{:S(2)}) copy-start(f32[256,64]{0,1:T(8,128)} %param.8) | copy-start | bytes 196612
  53.0 19.2 %collective-permute-start.6 = (bf16[256,256]{0,1:T(8,128)(2,1)S(1)}, bf16[256,256]{0,1:T(8,128)(2,1)S(1)}, u32[]{:S(2)}, u32[]{:S(2)}) collective-permute-start(bf16[256,256]{0,1:T(8,128)(2,1)S(1)} %get-tuple-element.17), channel_id=1, source_target_pairs={{0,4},{4,8},{8,12},{12,16},{16,20},{20,24},{24,28},{28,32},{32,36}... | collective-permute-start | bytes 393224 | tf_op jit(solution)/shard_map/ppermute | solution.py:21
  57.5 18.9 %collective-permute-start.11 = (bf16[256,256]{0,1:T(8,128)(2,1)S(1)}, bf16[256,256]{0,1:T(8,128)(2,1)S(1)}, u32[]{:S(2)}, u32[]{:S(2)}) collective-permute-start(bf16[256,256]{0,1:T(8,128)(2,1)S(1)} %get-tuple-element.18), channel_id=1, source_target_pairs={{0,24},{4,28},{8,32},{12,36},{16,40},{20,44},{24,48},{28,52},{32,5... | collective-permute-start | bytes 393224 | tf_op jit(solution)/shard_map/ppermute | solution.py:21
  59.6 16.8 %collective-permute-start.10 = (bf16[256,256]{0,1:T(8,128)(2,1)S(1)}, bf16[256,256]{0,1:T(8,128)(2,1)S(1)}, u32[]{:S(2)}, u32[]{:S(2)}) collective-permute-start(bf16[256,256]{0,1:T(8,128)(2,1)S(1)} %get-tuple-element.19), channel_id=1, source_target_pairs={{0,20},{4,24},{8,28},{12,32},{16,36},{20,40},{24,44},{28,48},{32,5... | collective-permute-start | bytes 393224 | tf_op jit(solution)/shard_map/ppermute | solution.py:21
  61.5 14.9 %collective-permute-start.9 = (bf16[256,256]{0,1:T(8,128)(2,1)S(1)}, bf16[256,256]{0,1:T(8,128)(2,1)S(1)}, u32[]{:S(2)}, u32[]{:S(2)}) collective-permute-start(bf16[256,256]{0,1:T(8,128)(2,1)S(1)} %get-tuple-element.20), channel_id=1, source_target_pairs={{0,16},{4,20},{8,24},{12,28},{16,32},{20,36},{24,40},{28,44},{32,4... | collective-permute-start | bytes 393224 | tf_op jit(solution)/shard_map/ppermute | solution.py:21
  66.9 9.6 %collective-permute-start.8 = (bf16[256,256]{0,1:T(8,128)(2,1)S(1)}, bf16[256,256]{0,1:T(8,128)(2,1)S(1)}, u32[]{:S(2)}, u32[]{:S(2)}) collective-permute-start(bf16[256,256]{0,1:T(8,128)(2,1)S(1)} %get-tuple-element.21), channel_id=1, source_target_pairs={{0,12},{4,16},{8,20},{12,24},{16,28},{20,32},{24,36},{28,40},{32,4... | collective-permute-start | bytes 393224 | tf_op jit(solution)/shard_map/ppermute | solution.py:21
  72.2 9.2 %copy-start.1 = (bf16[256,256]{0,1:T(8,128)(2,1)}, bf16[256,256]{0,1:T(8,128)(2,1)S(1)}, u32[]{:S(2)}) copy-start(bf16[256,256]{0,1:T(8,128)(2,1)S(1)} %collective-permute-done.6) | copy-start | bytes 393220
  72.2 9.1 %collective-permute-start.7 = (bf16[256,256]{0,1:T(8,128)(2,1)S(1)}, bf16[256,256]{0,1:T(8,128)(2,1)S(1)}, u32[]{:S(2)}, u32[]{:S(2)}) collective-permute-start(bf16[256,256]{0,1:T(8,128)(2,1)S(1)} %get-tuple-element.22), channel_id=1, source_target_pairs={{0,8},{4,12},{8,16},{12,20},{16,24},{20,28},{24,32},{28,36},{32,40... | collective-permute-start | bytes 393224 | tf_op jit(solution)/shard_map/ppermute | solution.py:21
  76.4 5.0 %copy-start.2 = (bf16[256,256]{0,1:T(8,128)(2,1)}, bf16[256,256]{0,1:T(8,128)(2,1)S(1)}, u32[]{:S(2)}) copy-start(bf16[256,256]{0,1:T(8,128)(2,1)S(1)} %collective-permute-done.11) | copy-start | bytes 393220
  83.6 22.1 %collective-permute-start.12 = (bf16[256,256]{0,1:T(8,128)(2,1)S(1)}, bf16[256,256]{0,1:T(8,128)(2,1)S(1)}, u32[]{:S(2)}, u32[]{:S(2)}) collective-permute-start(bf16[256,256]{0,1:T(8,128)(2,1)S(1)} %get-tuple-element.6), channel_id=1, source_target_pairs={{4,0},{8,4},{12,8},{16,12},{20,16},{24,20},{28,24},{32,28},{36,32}... | collective-permute-start | bytes 393224 | tf_op jit(solution)/shard_map/ppermute | solution.py:21
  86.0 26.4 %collective-permute-start.17 = (bf16[256,256]{0,1:T(8,128)(2,1)S(1)}, bf16[256,256]{0,1:T(8,128)(2,1)S(1)}, u32[]{:S(2)}, u32[]{:S(2)}) collective-permute-start(bf16[256,256]{0,1:T(8,128)(2,1)S(1)} %get-tuple-element.6), channel_id=1, source_target_pairs={{24,0},{28,4},{32,8},{36,12},{40,16},{44,20},{48,24},{52,28},{56,3... | collective-permute-start | bytes 393224 | tf_op jit(solution)/shard_map/ppermute | solution.py:21
  88.5 23.8 %collective-permute-start.16 = (bf16[256,256]{0,1:T(8,128)(2,1)S(1)}, bf16[256,256]{0,1:T(8,128)(2,1)S(1)}, u32[]{:S(2)}, u32[]{:S(2)}) collective-permute-start(bf16[256,256]{0,1:T(8,128)(2,1)S(1)} %get-tuple-element.6), channel_id=1, source_target_pairs={{20,0},{24,4},{28,8},{32,12},{36,16},{40,20},{44,24},{48,28},{52,3... | collective-permute-start | bytes 393224 | tf_op jit(solution)/shard_map/ppermute | solution.py:21
  93.0 19.3 %collective-permute-start.15 = (bf16[256,256]{0,1:T(8,128)(2,1)S(1)}, bf16[256,256]{0,1:T(8,128)(2,1)S(1)}, u32[]{:S(2)}, u32[]{:S(2)}) collective-permute-start(bf16[256,256]{0,1:T(8,128)(2,1)S(1)} %get-tuple-element.6), channel_id=1, source_target_pairs={{16,0},{20,4},{24,8},{28,12},{32,16},{36,20},{40,24},{44,28},{48,3... | collective-permute-start | bytes 393224 | tf_op jit(solution)/shard_map/ppermute | solution.py:21
  95.4 16.8 %collective-permute-start.14 = (bf16[256,256]{0,1:T(8,128)(2,1)S(1)}, bf16[256,256]{0,1:T(8,128)(2,1)S(1)}, u32[]{:S(2)}, u32[]{:S(2)}) collective-permute-start(bf16[256,256]{0,1:T(8,128)(2,1)S(1)} %get-tuple-element.6), channel_id=1, source_target_pairs={{12,0},{16,4},{20,8},{24,12},{28,16},{32,20},{36,24},{40,28},{44,3... | collective-permute-start | bytes 393224 | tf_op jit(solution)/shard_map/ppermute | solution.py:21
  99.2 18.0 %all-to-all-start.1 = ((bf16[4,256,256]{2,1,0:T(8,128)(2,1)}), bf16[4,256,256]{2,1,0:T(8,128)(2,1)}, u32[]{:S(2)}, u32[]{:S(2)}) async-start(bf16[4,256,256]{2,1,0:T(8,128)(2,1)} %tile.11), calls=%async_computation.3 | async-start | bytes 1048576 | tf_op jit(solution)/shard_map/all_to_all | solution.py:13
  105.7 50.9 %reduce-scatter.5.cloned.1.call-start = ((), (), s32[]{:S(2)}) async-start(), calls=%async_computation.5 | async-start | bytes 655360 | tf_op jit(solution)/shard_map/reduce_scatter | solution.py:55
  105.7 6.5 %collective-permute-start.13 = (bf16[256,256]{0,1:T(8,128)(2,1)S(1)}, bf16[256,256]{0,1:T(8,128)(2,1)S(1)}, u32[]{:S(2)}, u32[]{:S(2)}) collective-permute-start(bf16[256,256]{0,1:T(8,128)(2,1)S(1)} %get-tuple-element.6), channel_id=1, source_target_pairs={{8,0},{12,4},{16,8},{20,12},{24,16},{28,20},{32,24},{36,28},{40,32... | collective-permute-start | bytes 393224 | tf_op jit(solution)/shard_map/ppermute | solution.py:21
  125.7 22.2 %collective-permute-start.18 = (bf16[256,256]{0,1:T(8,128)(2,1)S(1)}, bf16[256,256]{0,1:T(8,128)(2,1)S(1)}, u32[]{:S(2)}, u32[]{:S(2)}) collective-permute-start(bf16[256,256]{0,1:T(8,128)(2,1)S(1)} %get-tuple-element.11), channel_id=1, source_target_pairs={{0,4},{4,8},{8,12},{12,16},{16,20},{20,24},{24,28},{28,32},{32,36}... | collective-permute-start | bytes 393224 | tf_op jit(solution)/shard_map/ppermute | solution.py:21
  129.2 22.2 %collective-permute-start.23 = (bf16[256,256]{0,1:T(8,128)(2,1)S(1)}, bf16[256,256]{0,1:T(8,128)(2,1)S(1)}, u32[]{:S(2)}, u32[]{:S(2)}) collective-permute-start(bf16[256,256]{0,1:T(8,128)(2,1)S(1)} %get-tuple-element.12), channel_id=1, source_target_pairs={{0,24},{4,28},{8,32},{12,36},{16,40},{20,44},{24,48},{28,52},{32,5... | collective-permute-start | bytes 393224 | tf_op jit(solution)/shard_map/ppermute | solution.py:21
  135.3 16.1 %collective-permute-start.22 = (bf16[256,256]{0,1:T(8,128)(2,1)S(1)}, bf16[256,256]{0,1:T(8,128)(2,1)S(1)}, u32[]{:S(2)}, u32[]{:S(2)}) collective-permute-start(bf16[256,256]{0,1:T(8,128)(2,1)S(1)} %get-tuple-element.13), channel_id=1, source_target_pairs={{0,20},{4,24},{8,28},{12,32},{16,36},{20,40},{24,44},{28,48},{32,5... | collective-permute-start | bytes 393224 | tf_op jit(solution)/shard_map/ppermute | solution.py:21
  137.3 14.2 %collective-permute-start.21 = (bf16[256,256]{0,1:T(8,128)(2,1)S(1)}, bf16[256,256]{0,1:T(8,128)(2,1)S(1)}, u32[]{:S(2)}, u32[]{:S(2)}) collective-permute-start(bf16[256,256]{0,1:T(8,128)(2,1)S(1)} %get-tuple-element.14), channel_id=1, source_target_pairs={{0,16},{4,20},{8,24},{12,28},{16,32},{20,36},{24,40},{28,44},{32,4... | collective-permute-start | bytes 393224 | tf_op jit(solution)/shard_map/ppermute | solution.py:21
  142.1 11.4 %collective-permute-start.20 = (bf16[256,256]{0,1:T(8,128)(2,1)S(1)}, bf16[256,256]{0,1:T(8,128)(2,1)S(1)}, u32[]{:S(2)}, u32[]{:S(2)}) collective-permute-start(bf16[256,256]{0,1:T(8,128)(2,1)S(1)} %get-tuple-element.15), channel_id=1, source_target_pairs={{0,12},{4,16},{8,20},{12,24},{16,28},{20,32},{24,36},{28,40},{32,4... | collective-permute-start | bytes 393224 | tf_op jit(solution)/shard_map/ppermute | solution.py:21
  147.8 8.7 %collective-permute-start.19 = (bf16[256,256]{0,1:T(8,128)(2,1)S(1)}, bf16[256,256]{0,1:T(8,128)(2,1)S(1)}, u32[]{:S(2)}, u32[]{:S(2)}) collective-permute-start(bf16[256,256]{0,1:T(8,128)(2,1)S(1)} %get-tuple-element.16), channel_id=1, source_target_pairs={{0,8},{4,12},{8,16},{12,20},{16,24},{20,28},{24,32},{28,36},{32,40... | collective-permute-start | bytes 393224 | tf_op jit(solution)/shard_map/ppermute | solution.py:21
  (4 other events, 15.6 us)
Sparse Core Ops, SparseCore 0:
  49.8 29.9 reduce-scatter.2
  117.3 30.0 reduce-scatter.4
